TPU v7x, 128 devices: a whole 4x4x4 slice. The times are simulated.
128 devices in a mesh: dp: 16 (over z, y_hi, core), seq: 8 (over x, y_lo).
Axes of the slice: x: 4, y: 4 (y_hi: 2, y_lo: 2; y = y_hi * 2 + y_lo), z: 4, core: 2. Of those that a mesh axis runs over, the one named last changes fastest.
Arguments:
- streams: bfloat16 [3, 16, 2048, 512], P(None, 'dp', 'seq'), may hold values from -6 to 6
- short_filter: float32 [3, 3, 512], replicated, may hold values from -3 to 3
- long_filter: float32 [2048, 512], P('seq'), may hold values from -4 to 4
- skip_gain: float32 [512], replicated, may hold values from -4 to 4
- out_weight: bfloat16 [512, 4096], replicated, may hold values from -0.25 to 0.25
- out_grad: bfloat16 [16, 2048, 4096], P('dp', 'seq'), may hold values from -6 to 6
Outputs:
- layer_out: bfloat16 [16, 2048, 4096], P('dp', 'seq')
- grad_streams: bfloat16 [3, 16, 2048, 512], P(None, 'dp', 'seq')
- grad_filter: float32 [2048, 512], P('seq')
- grad_out_weight: float32 [512, 4096], replicated
All inputs are finite; a program needn't handle non-finite values.
Results may differ from a plain program's by a relative error of at most 0.0049.
Values may be sent and summed in bfloat16 or wider, within the bound.
No kernel may reach another device: no remote copies, remote signals or barrier semaphores. Data moves between devices by JAX's collectives and lax.ppermute only.
A program may use at most 128 MiB of HBM per device.

v0:
```python
import math
import jax
import jax.numpy as jnp
from jax import lax
from jax.sharding import PartitionSpec as P


def swapped(array, axis, apart):
    return lax.ppermute(array, axis, [(i, i ^ 1 << apart) for i in range(lax.axis_size(axis))])


def passed_along(block, axis, distance):
    devices = range(lax.axis_size(axis))
    route = [(i - distance, i) for i in devices if i - distance in devices]
    return lax.ppermute(block, axis, route)


def spectral_table(length_here):
    row_index = lax.broadcasted_iota(jnp.int32, (length_here, length_here), 0)
    col_index = lax.broadcasted_iota(jnp.int32, (length_here, length_here), 1)
    phase_angle = (row_index * col_index % length_here).astype(jnp.float32) * (
        2.0 * math.pi / length_here
    )
    return (jnp.cos(phase_angle), jnp.sin(phase_angle))


def table_apply(matrix, values, pattern):
    return jnp.einsum(pattern, matrix, values, precision=lax.Precision.HIGHEST)


def transform_along(real_part, imaginary, direction, pattern):
    cosine, sine_table = spectral_table(real_part.shape[1])
    cosine_real = table_apply(cosine, real_part, pattern)
    cosine_imaginary = table_apply(cosine, imaginary, pattern)
    sine_real = table_apply(sine_table, real_part, pattern)
    sine_imaginary = table_apply(sine_table, imaginary, pattern)
    return (cosine_real - direction * sine_imaginary, cosine_imaginary + direction * sine_real)


def rotate_complex(real_part, imaginary, cosine, sine_value):
    return (
        real_part * cosine - imaginary * sine_value,
        real_part * sine_value + imaginary * cosine,
    )


def branch_angle(start_row, block_rows, total_length):
    positions = start_row + lax.broadcasted_iota(jnp.int32, (1, block_rows, 1), 1)
    return positions.astype(jnp.float32) * (math.pi / total_length)


def padded_branches(signal, start_row, total_length):
    phase_angle = branch_angle(start_row, signal.shape[1], total_length)
    real_part = jnp.concatenate([signal, signal * jnp.cos(phase_angle)], axis=0)
    imaginary = jnp.concatenate([jnp.zeros_like(signal), -signal * jnp.sin(phase_angle)], axis=0)
    return (real_part, imaginary)


def combine_branches(real_part, imaginary, start_row, total_length):
    members = real_part.shape[0] // 2
    phase_angle = branch_angle(start_row, real_part.shape[1], total_length)
    return 0.5 * (
        real_part[:members]
        + jnp.cos(phase_angle) * real_part[members:]
        - jnp.sin(phase_angle) * imaginary[members:]
    )


def level_twiddle(position, split_bit, block_rows):
    half_span = block_rows * (1 << split_bit)
    within = position % (1 << split_bit) * block_rows + lax.broadcasted_iota(
        jnp.int32, (1, block_rows, 1), 1
    )
    phase_angle = within.astype(jnp.float32) * (math.pi / half_span)
    return (jnp.cos(phase_angle), -jnp.sin(phase_angle))


def forward_levels(real_part, imaginary):
    seq_count = lax.axis_size("seq")
    position = lax.axis_index("seq")
    block_rows = real_part.shape[1]
    for split_bit in reversed(range(seq_count.bit_length() - 1)):
        upper_half = position >> split_bit & 1 == 1
        cosine, sine_value = level_twiddle(position, split_bit, block_rows)
        other_real, other_imaginary = swapped((real_part, imaginary), "seq", split_bit)
        turned_real, turned_imaginary = rotate_complex(
            other_real - real_part, other_imaginary - imaginary, cosine, sine_value
        )
        real_part = jnp.where(upper_half, turned_real, real_part + other_real)
        imaginary = jnp.where(upper_half, turned_imaginary, imaginary + other_imaginary)
    return (real_part, imaginary)


def inverse_levels(real_part, imaginary):
    seq_count = lax.axis_size("seq")
    position = lax.axis_index("seq")
    block_rows = real_part.shape[1]
    for split_bit in range(seq_count.bit_length() - 1):
        upper_half = position >> split_bit & 1 == 1
        cosine, sine_value = level_twiddle(position, split_bit, block_rows)
        turned_real, turned_imaginary = rotate_complex(real_part, imaginary, cosine, -sine_value)
        own_real = jnp.where(upper_half, turned_real, real_part)
        own_imaginary = jnp.where(upper_half, turned_imaginary, imaginary)
        other_real, other_imaginary = swapped((own_real, own_imaginary), "seq", split_bit)
        real_part = 0.5 * jnp.where(upper_half, other_real - own_real, other_real + own_real)
        imaginary = 0.5 * jnp.where(
            upper_half, other_imaginary - own_imaginary, other_imaginary + own_imaginary
        )
    return (real_part, imaginary)


def forward_spectrum(signal, start_row, total_length):
    real_part, imaginary = padded_branches(signal, start_row, total_length)
    real_part, imaginary = forward_levels(real_part, imaginary)
    return transform_along(real_part, imaginary, -1.0, "js,msc->mjc")


def inverse_signal(real_part, imaginary, start_row, total_length):
    block_rows = real_part.shape[1]
    real_part, imaginary = transform_along(real_part, imaginary, 1.0, "js,msc->mjc")
    real_part = real_part / block_rows
    imaginary = imaginary / block_rows
    real_part, imaginary = inverse_levels(real_part, imaginary)
    return combine_branches(real_part, imaginary, start_row, total_length)


def on_device(streams, short_filter, long_filter, skip_gain, out_weight, out_grad):
    seq_count = lax.axis_size("seq")
    batch_here = streams.shape[1]
    block_rows = streams.shape[2]
    channels = streams.shape[3]
    total_length = block_rows * seq_count
    start_row = lax.axis_index("seq") * block_rows
    grad_scale = 1.0 / math.sqrt(batch_here * lax.axis_size("dp") * total_length)
    earlier = passed_along(streams[:, :, block_rows - 2 :, :], "seq", 1)
    extended = jnp.concatenate([earlier, streams], axis=2).astype(jnp.float32)
    shortened = sum(
        (
            short_filter[:, offset, None, None, :]
            * extended[:, :, 2 - offset : 2 - offset + block_rows, :]
            for offset in range(3)
        )
    )
    gate_out, gate_in, value_stream = (shortened[0], shortened[1], shortened[2])
    product = gate_in * value_stream
    members = batch_here + 1
    spectrum_real, spectrum_imaginary = forward_spectrum(
        jnp.concatenate([product, long_filter[None]], axis=0), start_row, total_length
    )
    spectrum_real = spectrum_real.reshape(2, members, block_rows, channels)
    spectrum_imaginary = spectrum_imaginary.reshape(2, members, block_rows, channels)
    product_real, product_imaginary = (
        spectrum_real[:, :batch_here],
        spectrum_imaginary[:, :batch_here],
    )
    filter_real, filter_imaginary = (
        spectrum_real[:, batch_here:],
        spectrum_imaginary[:, batch_here:],
    )
    conv_real = product_real * filter_real - product_imaginary * filter_imaginary
    conv_imaginary = product_real * filter_imaginary + product_imaginary * filter_real
    convolved = inverse_signal(
        conv_real.reshape(2 * batch_here, block_rows, channels),
        conv_imaginary.reshape(2 * batch_here, block_rows, channels),
        start_row,
        total_length,
    )
    convolved = convolved + skip_gain * product
    mixed_out = (gate_out * convolved).astype(jnp.bfloat16)
    mixed_flat = mixed_out.reshape(batch_here * block_rows, channels)
    grad_flat = out_grad.reshape(batch_here * block_rows, out_grad.shape[2])
    layer_out = (
        jnp.dot(mixed_flat, out_weight, preferred_element_type=jnp.float32)
        .astype(jnp.bfloat16)
        .reshape(out_grad.shape)
    )
    grad_mixed = lax.dot_general(
        grad_flat, out_weight, (((1,), (1,)), ((), ())), preferred_element_type=jnp.float32
    ).reshape(batch_here, block_rows, channels)
    grad_conv = grad_mixed * gate_out
    grad_gate_out = grad_mixed * convolved
    grad_real, grad_imaginary = forward_spectrum(grad_conv, start_row, total_length)
    grad_real = grad_real.reshape(2, batch_here, block_rows, channels)
    grad_imaginary = grad_imaginary.reshape(2, batch_here, block_rows, channels)
    back_real = filter_real * grad_real + filter_imaginary * grad_imaginary
    back_imaginary = filter_real * grad_imaginary - filter_imaginary * grad_real
    lag_real = jnp.sum(
        product_real * grad_real + product_imaginary * grad_imaginary, axis=1, keepdims=True
    )
    lag_imaginary = jnp.sum(
        product_real * grad_imaginary - product_imaginary * grad_real, axis=1, keepdims=True
    )
    joined_real = jnp.concatenate([back_real, lag_real], axis=1).reshape(
        2 * members, block_rows, channels
    )
    joined_imaginary = jnp.concatenate([back_imaginary, lag_imaginary], axis=1).reshape(
        2 * members, block_rows, channels
    )
    inverse_rows = inverse_signal(joined_real, joined_imaginary, start_row, total_length)
    grad_product = inverse_rows[:batch_here] + skip_gain * grad_conv
    filter_part = inverse_rows[batch_here]
    grad_shortened = jnp.stack([grad_gate_out, grad_product * value_stream, grad_product * gate_in])
    later_rows = passed_along(grad_shortened[:, :, :2, :], "seq", -1)
    extended_grad = jnp.concatenate([grad_shortened, later_rows], axis=2)
    grad_streams = sum(
        (
            short_filter[:, offset, None, None, :]
            * extended_grad[:, :, offset : offset + block_rows, :]
            for offset in range(3)
        )
    )
    partial_value = lax.dot_general(
        mixed_flat, grad_flat, (((0,), (0,)), ((), ())), preferred_element_type=jnp.float32
    )
    grad_out_weight = lax.psum(partial_value, ("dp", "seq")) * grad_scale
    grad_filter = lax.psum(filter_part, "dp") * grad_scale
    return (layer_out, grad_streams.astype(jnp.bfloat16), grad_filter, grad_out_weight)


def solution(mesh):
    placed = (P(None, "dp", "seq", None), P(), P("seq", None), P(), P(), P("dp", "seq", None))
    return jax.shard_map(
        on_device,
        mesh=mesh,
        in_specs=placed,
        out_specs=(P("dp", "seq", None), P(None, "dp", "seq", None), P("seq", None), P()),
        check_vma=False,
    )
```

profile of v0, /device:TPU:1, one launch (start us, length us, event | category | flops | bytes accessed | tf_op | source)
XLA Modules:
  0.0 1175.4 jit_solution(6477687003662021271)
XLA Ops:
  31.0 34.8 %collective-permute-done.1 = f32[4,256,512]{2,1,0:T(8,128)} collective-permute-done((f32[4,256,512]{2,1,0:T(8,128)}, f32[4,256,512]{2,1,0:T(8,128)}, u32[]{:S(2)}, u32[]{:S(2)}) %collective-permute-start.1) | collective-permute-done | bytes 2097184 | tf_op jit(solution)/shard_map/ppermute | solution.py:9
  65.7 44.9 %collective-permute-done.2 = f32[4,256,512]{2,1,0:T(8,128)} collective-permute-done((f32[4,256,512]{2,1,0:T(8,128)}, f32[4,256,512]{2,1,0:T(8,128)}, u32[]{:S(2)}, u32[]{:S(2)}) %collective-permute-start.2) | collective-permute-done | bytes 2097184 | tf_op jit(solution)/shard_map/ppermute | solution.py:9
  118.4 14.8 %collective-permute-done.13 = f32[2,256,512]{2,1,0:T(8,128)} collective-permute-done((f32[2,256,512]{2,1,0:T(8,128)}, f32[2,256,512]{2,1,0:T(8,128)}, u32[]{:S(2)}, u32[]{:S(2)}) %collective-permute-start.13) | collective-permute-done | bytes 1048608 | tf_op jit(solution)/shard_map/ppermute | solution.py:9
  133.1 22.5 %collective-permute-done.14 = f32[2,256,512]{2,1,0:T(8,128)} collective-permute-done((f32[2,256,512]{2,1,0:T(8,128)}, f32[2,256,512]{2,1,0:T(8,128)}, u32[]{:S(2)}, u32[]{:S(2)}) %collective-permute-start.14) | collective-permute-done | bytes 1048608 | tf_op jit(solution)/shard_map/ppermute | solution.py:9
  160.6 107.4 %collective-permute-done.15 = f32[2,256,512]{2,1,0:T(8,128)} collective-permute-done((f32[2,256,512]{2,1,0:T(8,128)}, f32[2,256,512]{2,1,0:T(8,128)}, u32[]{:S(2)}, u32[]{:S(2)}) %collective-permute-start.15) | collective-permute-done | bytes 1048608 | tf_op jit(solution)/shard_map/ppermute | solution.py:9
  268.0 22.5 %collective-permute-done.16 = f32[2,256,512]{2,1,0:T(8,128)} collective-permute-done((f32[2,256,512]{2,1,0:T(8,128)}, f32[2,256,512]{2,1,0:T(8,128)}, u32[]{:S(2)}, u32[]{:S(2)}) %collective-permute-start.16) | collective-permute-done | bytes 1048608 | tf_op jit(solution)/shard_map/ppermute | solution.py:9
  296.1 6.7 add_select_fusion.7
  304.8 12.0 %collective-permute-done.17 = f32[2,256,512]{2,1,0:T(8,128)} collective-permute-done((f32[2,256,512]{2,1,0:T(8,128)}, f32[2,256,512]{2,1,0:T(8,128)}, u32[]{:S(2)}, u32[]{:S(2)}) %collective-permute-start.17) | collective-permute-done | bytes 1048608 | tf_op jit(solution)/shard_map/ppermute | solution.py:9
  316.8 22.5 %collective-permute-done.18 = f32[2,256,512]{2,1,0:T(8,128)} collective-permute-done((f32[2,256,512]{2,1,0:T(8,128)}, f32[2,256,512]{2,1,0:T(8,128)}, u32[]{:S(2)}, u32[]{:S(2)}) %collective-permute-start.18) | collective-permute-done | bytes 1048608 | tf_op jit(solution)/shard_map/ppermute | solution.py:9
  350.0 34.2 %collective-permute-done.5 = f32[4,256,512]{2,1,0:T(8,128)} collective-permute-done((f32[4,256,512]{2,1,0:T(8,128)}, f32[4,256,512]{2,1,0:T(8,128)}, u32[]{:S(2)}, u32[]{:S(2)}) %collective-permute-start.5) | collective-permute-done | bytes 2097184 | tf_op jit(solution)/shard_map/ppermute | solution.py:9
  384.2 44.9 %collective-permute-done.6 = f32[4,256,512]{2,1,0:T(8,128)} collective-permute-done((f32[4,256,512]{2,1,0:T(8,128)}, f32[4,256,512]{2,1,0:T(8,128)}, u32[]{:S(2)}, u32[]{:S(2)}) %collective-permute-start.6) | collective-permute-done | bytes 2097184 | tf_op jit(solution)/shard_map/ppermute | solution.py:9
  452.4 6.3 multiply_subtract_fusion.2
  492.1 35.7 %collective-permute-done.19 = f32[4,256,512]{2,1,0:T(8,128)S(1)} collective-permute-done((f32[4,256,512]{2,1,0:T(8,128)S(1)}, f32[4,256,512]{2,1,0:T(8,128)S(1)}, u32[]{:S(2)}, u32[]{:S(2)}) %collective-permute-start.19) | collective-permute-done | bytes 2097184 | tf_op jit(solution)/shard_map/ppermute | solution.py:9
  527.8 44.9 %collective-permute-done.20 = f32[4,256,512]{2,1,0:T(8,128)S(1)} collective-permute-done((f32[4,256,512]{2,1,0:T(8,128)S(1)}, f32[4,256,512]{2,1,0:T(8,128)S(1)}, u32[]{:S(2)}, u32[]{:S(2)}) %collective-permute-start.20) | collective-permute-done | bytes 2097184 | tf_op jit(solution)/shard_map/ppermute | solution.py:9
  580.0 18.0 %collective-permute-done.7 = f32[2,256,512]{2,1,0:T(8,128)S(1)} collective-permute-done((f32[2,256,512]{2,1,0:T(8,128)S(1)}, f32[2,256,512]{2,1,0:T(8,128)S(1)}, u32[]{:S(2)}, u32[]{:S(2)}) %collective-permute-start.7) | collective-permute-done | bytes 1048608 | tf_op jit(solution)/shard_map/ppermute | solution.py:9
  598.0 22.5 %collective-permute-done.8 = f32[2,256,512]{2,1,0:T(8,128)S(1)} collective-permute-done((f32[2,256,512]{2,1,0:T(8,128)S(1)}, f32[2,256,512]{2,1,0:T(8,128)S(1)}, u32[]{:S(2)}, u32[]{:S(2)}) %collective-permute-start.8) | collective-permute-done | bytes 1048608 | tf_op jit(solution)/shard_map/ppermute | solution.py:9
  622.7 39.0 %collective-permute-done.22 = f32[4,256,512]{2,1,0:T(8,128)S(1)} collective-permute-done((f32[4,256,512]{2,1,0:T(8,128)S(1)}, f32[4,256,512]{2,1,0:T(8,128)S(1)}, u32[]{:S(2)}, u32[]{:S(2)}) %collective-permute-start.22) | collective-permute-done | bytes 2097184 | tf_op jit(solution)/shard_map/ppermute | solution.py:9
  666.3 17.9 %collective-permute-done.10 = f32[2,256,512]{2,1,0:T(8,128)S(1)} collective-permute-done((f32[2,256,512]{2,1,0:T(8,128)S(1)}, f32[2,256,512]{2,1,0:T(8,128)S(1)}, u32[]{:S(2)}, u32[]{:S(2)}) %collective-permute-start.10) | collective-permute-done | bytes 1048608 | tf_op jit(solution)/shard_map/ppermute | solution.py:9
  684.2 22.5 %collective-permute-done.9 = f32[2,256,512]{2,1,0:T(8,128)S(1)} collective-permute-done((f32[2,256,512]{2,1,0:T(8,128)S(1)}, f32[2,256,512]{2,1,0:T(8,128)S(1)}, u32[]{:S(2)}, u32[]{:S(2)}) %collective-permute-start.9) | collective-permute-done | bytes 1048608 | tf_op jit(solution)/shard_map/ppermute | solution.py:9
  710.5 109.4 %collective-permute-done.11 = f32[2,256,512]{2,1,0:T(8,128)S(1)} collective-permute-done((f32[2,256,512]{2,1,0:T(8,128)S(1)}, f32[2,256,512]{2,1,0:T(8,128)S(1)}, u32[]{:S(2)}, u32[]{:S(2)}) %collective-permute-start.11) | collective-permute-done | bytes 1048608 | tf_op jit(solution)/shard_map/ppermute | solution.py:9
  820.2 22.2 %collective-permute-done.12 = f32[2,256,512]{2,1,0:T(8,128)S(1)} collective-permute-done((f32[2,256,512]{2,1,0:T(8,128)S(1)}, f32[2,256,512]{2,1,0:T(8,128)S(1)}, u32[]{:S(2)}, u32[]{:S(2)}) %collective-permute-start.12) | collective-permute-done | bytes 1048608 | tf_op jit(solution)/shard_map/ppermute | solution.py:9
  860.8 130.1 %all-reduce.5.cloned.1.call-done = f32[256,512]{1,0:T(8,128)} async-done(((f32[256,512]{1,0:T(8,128)}), f32[256,512]{1,0:T(8,128)}) %all-reduce.5.cloned.1.call-update) | async-done | bytes 524304 | tf_op jit(solution)/shard_map/psum | solution.py:216
  992.7 167.3 %all-reduce.7.cloned.1.call-done = f32[512,4096]{1,0:T(8,128)} async-done(((f32[512,4096]{1,0:T(8,128)}), f32[512,4096]{1,0:T(8,128)}) %all-reduce.7.cloned.1.call-update) | async-done | bytes 8388624 | tf_op jit(solution)/shard_map/psum | solution.py:215
  1160.1 8.3 broadcast_multiply_fusion
  (140 shorter events, 149.3 us)
Async XLA Ops:
  7.2 983.7 %all-reduce.5.cloned.1.call-start = ((), (), s32[]{:S(2)}) async-start(), calls=%async_computation | async-start | bytes 1048576 | tf_op jit(solution)/shard_map/psum | solution.py:216
  17.5 48.2 %collective-permute-start.1 = (f32[4,256,512]{2,1,0:T(8,128)}, f32[4,256,512]{2,1,0:T(8,128)}, u32[]{:S(2)}, u32[]{:S(2)}) collective-permute-start(f32[4,256,512]{2,1,0:T(8,128)} %pad_maximum_fusion), channel_id=1, source_target_pairs={{0,4},{1,5},{2,6},{3,7},{4,0},{5,1},{6,2},{7,3},{8,12},{9,13},{10,... | collective-permute-start | bytes 6291464 | tf_op jit(solution)/shard_map/ppermute | solution.py:9
  22.9 87.8 %collective-permute-start.2 = (f32[4,256,512]{2,1,0:T(8,128)}, f32[4,256,512]{2,1,0:T(8,128)}, u32[]{:S(2)}, u32[]{:S(2)}) collective-permute-start(f32[4,256,512]{2,1,0:T(8,128)} %concatenate.47), channel_id=1, source_target_pairs={{0,4},{1,5},{2,6},{3,7},{4,0},{5,1},{6,2},{7,3},{8,12},{9,13},{10,... | collective-permute-start | bytes 6291464 | tf_op jit(solution)/shard_map/ppermute | solution.py:9
  26.8 106.3 %collective-permute-start.13 = (f32[2,256,512]{2,1,0:T(8,128)}, f32[2,256,512]{2,1,0:T(8,128)}, u32[]{:S(2)}, u32[]{:S(2)}) collective-permute-start(f32[2,256,512]{2,1,0:T(8,128)} %pad_maximum_fusion.6), channel_id=1, source_target_pairs={{0,4},{1,5},{2,6},{3,7},{4,0},{5,1},{6,2},{7,3},{8,12},{9,13},{10,... | collective-permute-start | bytes 3145736 | tf_op jit(solution)/shard_map/ppermute | solution.py:9
  30.5 125.1 %collective-permute-start.14 = (f32[2,256,512]{2,1,0:T(8,128)}, f32[2,256,512]{2,1,0:T(8,128)}, u32[]{:S(2)}, u32[]{:S(2)}) collective-permute-start(f32[2,256,512]{2,1,0:T(8,128)} %concatenate.49), channel_id=1, source_target_pairs={{0,4},{1,5},{2,6},{3,7},{4,0},{5,1},{6,2},{7,3},{8,12},{9,13},{10,... | collective-permute-start | bytes 3145736 | tf_op jit(solution)/shard_map/ppermute | solution.py:9
  116.9 179.2 %collective-permute-start.3 = (f32[4,256,512]{2,1,0:T(8,128)}, f32[4,256,512]{2,1,0:T(8,128)}, u32[]{:S(2)}, u32[]{:S(2)}) collective-permute-start(f32[4,256,512]{2,1,0:T(8,128)} %get-tuple-element.16), channel_id=1, source_target_pairs={{0,2},{1,3},{2,0},{3,1},{4,6},{5,7},{6,4},{7,5},{8,10},{9,11},{10,... | collective-permute-start | bytes 6291464 | tf_op jit(solution)/shard_map/ppermute | solution.py:9
  118.0 178.0 %collective-permute-start.4 = (f32[4,256,512]{2,1,0:T(8,128)}, f32[4,256,512]{2,1,0:T(8,128)}, u32[]{:S(2)}, u32[]{:S(2)}) collective-permute-start(f32[4,256,512]{2,1,0:T(8,128)} %get-tuple-element.17), channel_id=1, source_target_pairs={{0,2},{1,3},{2,0},{3,1},{4,6},{5,7},{6,4},{7,5},{8,10},{9,11},{10,... | collective-permute-start | bytes 6291464 | tf_op jit(solution)/shard_map/ppermute | solution.py:9
  159.1 108.9 %collective-permute-start.15 = (f32[2,256,512]{2,1,0:T(8,128)}, f32[2,256,512]{2,1,0:T(8,128)}, u32[]{:S(2)}, u32[]{:S(2)}) collective-permute-start(f32[2,256,512]{2,1,0:T(8,128)} %get-tuple-element.35), channel_id=1, source_target_pairs={{0,2},{1,3},{2,0},{3,1},{4,6},{5,7},{6,4},{7,5},{8,10},{9,11},{10,... | collective-permute-start | bytes 3145736 | tf_op jit(solution)/shard_map/ppermute | solution.py:9
  160.2 130.2 %collective-permute-start.16 = (f32[2,256,512]{2,1,0:T(8,128)}, f32[2,256,512]{2,1,0:T(8,128)}, u32[]{:S(2)}, u32[]{:S(2)}) collective-permute-start(f32[2,256,512]{2,1,0:T(8,128)} %get-tuple-element.34), channel_id=1, source_target_pairs={{0,2},{1,3},{2,0},{3,1},{4,6},{5,7},{6,4},{7,5},{8,10},{9,11},{10,... | collective-permute-start | bytes 3145736 | tf_op jit(solution)/shard_map/ppermute | solution.py:9
  295.0 44.3 %collective-permute-start.18 = (f32[2,256,512]{2,1,0:T(8,128)}, f32[2,256,512]{2,1,0:T(8,128)}, u32[]{:S(2)}, u32[]{:S(2)}) collective-permute-start(f32[2,256,512]{2,1,0:T(8,128)} %get-tuple-element.26), channel_id=1, source_target_pairs={{0,1},{1,0},{2,3},{3,2},{4,5},{5,4},{6,7},{7,6},{8,9},{9,8},{10,11... | collective-permute-start | bytes 3145736 | tf_op jit(solution)/shard_map/ppermute | solution.py:9
  302.7 81.5 %collective-permute-start.5 = (f32[4,256,512]{2,1,0:T(8,128)}, f32[4,256,512]{2,1,0:T(8,128)}, u32[]{:S(2)}, u32[]{:S(2)}) collective-permute-start(f32[4,256,512]{2,1,0:T(8,128)} %get-tuple-element.14), channel_id=1, source_target_pairs={{0,1},{1,0},{2,3},{3,2},{4,5},{5,4},{6,7},{7,6},{8,9},{9,8},{10,11... | collective-permute-start | bytes 6291464 | tf_op jit(solution)/shard_map/ppermute | solution.py:9
  303.1 126.0 %collective-permute-start.6 = (f32[4,256,512]{2,1,0:T(8,128)}, f32[4,256,512]{2,1,0:T(8,128)}, u32[]{:S(2)}, u32[]{:S(2)}) collective-permute-start(f32[4,256,512]{2,1,0:T(8,128)} %get-tuple-element.15), channel_id=1, source_target_pairs={{0,1},{1,0},{2,3},{3,2},{4,5},{5,4},{6,7},{7,6},{8,9},{9,8},{10,11... | collective-permute-start | bytes 6291464 | tf_op jit(solution)/shard_map/ppermute | solution.py:9
  484.3 43.5 %collective-permute-start.19 = (f32[4,256,512]{2,1,0:T(8,128)S(1)}, f32[4,256,512]{2,1,0:T(8,128)S(1)}, u32[]{:S(2)}, u32[]{:S(2)}) collective-permute-start(f32[4,256,512]{2,1,0:T(8,128)S(1)} %get-tuple-element.23), channel_id=1, source_target_pairs={{0,1},{1,0},{2,3},{3,2},{4,5},{5,4},{6,7},{7,6},{8,9},{9,8},{10,11... | collective-permute-start | bytes 6291464 | tf_op jit(solution)/shard_map/ppermute | solution.py:9
  484.7 88.0 %collective-permute-start.20 = (f32[4,256,512]{2,1,0:T(8,128)S(1)}, f32[4,256,512]{2,1,0:T(8,128)S(1)}, u32[]{:S(2)}, u32[]{:S(2)}) collective-permute-start(f32[4,256,512]{2,1,0:T(8,128)S(1)} %get-tuple-element.22), channel_id=1, source_target_pairs={{0,1},{1,0},{2,3},{3,2},{4,5},{5,4},{6,7},{7,6},{8,9},{9,8},{10,11... | collective-permute-start | bytes 6291464 | tf_op jit(solution)/shard_map/ppermute | solution.py:9
  574.2 48.5 %collective-permute-start.21 = (f32[4,256,512]{2,1,0:T(8,128)S(1)}, f32[4,256,512]{2,1,0:T(8,128)S(1)}, u32[]{:S(2)}, u32[]{:S(2)}) collective-permute-start(f32[4,256,512]{2,1,0:T(8,128)S(1)} %get-tuple-element.11), channel_id=1, source_target_pairs={{0,2},{1,3},{2,0},{3,1},{4,6},{5,7},{6,4},{7,5},{8,10},{9,11},{10,... | collective-permute-start | bytes 6291464 | tf_op jit(solution)/shard_map/ppermute | solution.py:9
  575.5 86.3 %collective-permute-start.22 = (f32[4,256,512]{2,1,0:T(8,128)S(1)}, f32[4,256,512]{2,1,0:T(8,128)S(1)}, u32[]{:S(2)}, u32[]{:S(2)}) collective-permute-start(f32[4,256,512]{2,1,0:T(8,128)S(1)} %get-tuple-element.10), channel_id=1, source_target_pairs={{0,2},{1,3},{2,0},{3,1},{4,6},{5,7},{6,4},{7,5},{8,10},{9,11},{10,... | collective-permute-start | bytes 6291464 | tf_op jit(solution)/shard_map/ppermute | solution.py:9
  578.9 41.6 %collective-permute-start.8 = (f32[2,256,512]{2,1,0:T(8,128)S(1)}, f32[2,256,512]{2,1,0:T(8,128)S(1)}, u32[]{:S(2)}, u32[]{:S(2)}) collective-permute-start(f32[2,256,512]{2,1,0:T(8,128)S(1)} %get-tuple-element.38), channel_id=1, source_target_pairs={{0,1},{1,0},{2,3},{3,2},{4,5},{5,4},{6,7},{7,6},{8,9},{9,8},{10,11... | collective-permute-start | bytes 3145736 | tf_op jit(solution)/shard_map/ppermute | solution.py:9
  621.1 63.1 %collective-permute-start.10 = (f32[2,256,512]{2,1,0:T(8,128)S(1)}, f32[2,256,512]{2,1,0:T(8,128)S(1)}, u32[]{:S(2)}, u32[]{:S(2)}) collective-permute-start(f32[2,256,512]{2,1,0:T(8,128)S(1)} %get-tuple-element.30), channel_id=1, source_target_pairs={{0,2},{1,3},{2,0},{3,1},{4,6},{5,7},{6,4},{7,5},{8,10},{9,11},{10,... | collective-permute-start | bytes 3145736 | tf_op jit(solution)/shard_map/ppermute | solution.py:9
  622.4 84.3 %collective-permute-start.9 = (f32[2,256,512]{2,1,0:T(8,128)S(1)}, f32[2,256,512]{2,1,0:T(8,128)S(1)}, u32[]{:S(2)}, u32[]{:S(2)}) collective-permute-start(f32[2,256,512]{2,1,0:T(8,128)S(1)} %get-tuple-element.31), channel_id=1, source_target_pairs={{0,2},{1,3},{2,0},{3,1},{4,6},{5,7},{6,4},{7,5},{8,10},{9,11},{10,... | collective-permute-start | bytes 3145736 | tf_op jit(solution)/shard_map/ppermute | solution.py:9
  663.3 180.2 %collective-permute-start.23 = (f32[4,256,512]{2,1,0:T(8,128)S(1)}, f32[4,256,512]{2,1,0:T(8,128)S(1)}, u32[]{:S(2)}, u32[]{:S(2)}) collective-permute-start(f32[4,256,512]{2,1,0:T(8,128)S(1)} %get-tuple-element.9), channel_id=1, source_target_pairs={{0,4},{1,5},{2,6},{3,7},{4,0},{5,1},{6,2},{7,3},{8,12},{9,13},{10,... | collective-permute-start | bytes 6291464 | tf_op jit(solution)/shard_map/ppermute | solution.py:9
  665.1 178.9 %collective-permute-start.24 = (f32[4,256,512]{2,1,0:T(8,128)S(1)}, f32[4,256,512]{2,1,0:T(8,128)S(1)}, u32[]{:S(2)}, u32[]{:S(2)}) collective-permute-start(f32[4,256,512]{2,1,0:T(8,128)S(1)} %get-tuple-element.8), channel_id=1, source_target_pairs={{0,4},{1,5},{2,6},{3,7},{4,0},{5,1},{6,2},{7,3},{8,12},{9,13},{10,... | collective-permute-start | bytes 6291464 | tf_op jit(solution)/shard_map/ppermute | solution.py:9
  707.4 112.5 %collective-permute-start.11 = (f32[2,256,512]{2,1,0:T(8,128)S(1)}, f32[2,256,512]{2,1,0:T(8,128)S(1)}, u32[]{:S(2)}, u32[]{:S(2)}) collective-permute-start(f32[2,256,512]{2,1,0:T(8,128)S(1)} %get-tuple-element.28), channel_id=1, source_target_pairs={{0,4},{1,5},{2,6},{3,7},{4,0},{5,1},{6,2},{7,3},{8,12},{9,13},{10,... | collective-permute-start | bytes 3145736 | tf_op jit(solution)/shard_map/ppermute | solution.py:9
  709.2 133.1 %collective-permute-start.12 = (f32[2,256,512]{2,1,0:T(8,128)S(1)}, f32[2,256,512]{2,1,0:T(8,128)S(1)}, u32[]{:S(2)}, u32[]{:S(2)}) collective-permute-start(f32[2,256,512]{2,1,0:T(8,128)S(1)} %get-tuple-element.29), channel_id=1, source_target_pairs={{0,4},{1,5},{2,6},{3,7},{4,0},{5,1},{6,2},{7,3},{8,12},{9,13},{10,... | collective-permute-start | bytes 3145736 | tf_op jit(solution)/shard_map/ppermute | solution.py:9
  845.8 314.3 %all-reduce.7.cloned.1.call-start = ((), (), s32[]{:S(2)}) async-start(), calls=%async_computation.1 | async-start | bytes 16777216 | tf_op jit(solution)/shard_map/psum | solution.py:215
  (24 other events, 623.4 us)
Sparse Core Ops, SparseCore 0:
  845.9 144.8 all-reduce.4
  997.3 162.7 all-reduce.6
where the time goes:
time: 1180 us
  waiting for transfers between devices  990 us (84%)
  matrix products  67.5 us (6%)
  other arithmetic  58.3 us (5%)
  starting transfers between devices  31.8 us (3%)
  between operations  14.8 us (1%)
  local copies, waits for them, and re-layouts  12.9 us (1%)
    ppermute x24, waiting for transfers between devices, swapped(): lax.ppermute(array, axis, [(i, i ^ 1 << apart) for i in range(lax.axis_si...  693 us
    psum x1, waiting for transfers between devices, on_device(): grad_out_weight = lax.psum(partial_value, ('dp', 'seq')) * grad_scale  167 us
    psum x1, waiting for transfers between devices, on_device(): grad_filter = lax.psum(filter_part, 'dp') * grad_scale  130 us
    dot_general x16, matrix products, table_apply(): return jnp.einsum(pattern, matrix, values, precision=lax.Precision.HIGHEST)  56.8 us
    ppermute x24, starting transfers between devices, swapped(): lax.ppermute(array, axis, [(i, i ^ 1 << apart) for i in range(lax.axis_si...  26 us
  transfers between devices with their start and end apart: 28, of which 21 were waited for; matrix products, arithmetic and copies ran while one was open for 6% of the time, Pallas kernels for 0%

commit v1 on v0

--- a/solution.py
+++ b/solution.py
@@ -213,7 +213,7 @@
         mixed_flat, grad_flat, (((0,), (0,)), ((), ())), preferred_element_type=jnp.float32
     )
     grad_out_weight = lax.psum(partial_value, ("dp", "seq")) * grad_scale
-    grad_filter = lax.psum(filter_part, "dp") * grad_scale
+    grad_filter = jnp.sum(jax.lax.all_gather(filter_part, "dp"), axis=0) * grad_scale
     return (layer_out, grad_streams.astype(jnp.bfloat16), grad_filter, grad_out_weight)
 
 

time: 1180 us -> 1080 us (0.915)
  waiting for transfers between devices: 990 us -> 882 us
    psum x1 -> x0, waiting for transfers between devices: 130 us -> none  [on_device(): grad_filter = lax.psum(filter_part, 'dp') * grad_scale]
    psum x1, waiting for transfers between devices: 167 us -> 187 us  [on_device(): grad_out_weight = lax.psum(partial_value, ('dp', 'seq')) * grad_scale]
  transfers between devices with their start and end apart: 28 -> 28, of which waited for: 21 -> 20; matrix products, arithmetic and copies ran while one was open for 6% -> 6% of each run, Pallas kernels for 0% -> 0%
where the time goes in v1:
time: 1080 us; the launch traced here: 1070 us
  waiting for transfers between devices  882 us (82%)
  matrix products  70.1 us (6%)
  other arithmetic  60.2 us (6%)
  starting transfers between devices  31.3 us (3%)
  between operations  16.3 us (2%)
  local copies, waits for them, and re-layouts  13.1 us (1%)
    ppermute x24, waiting for transfers between devices, swapped(): lax.ppermute(array, axis, [(i, i ^ 1 << apart) for i in range(lax.axis_si...  695 us
    psum x1, waiting for transfers between devices, on_device(): grad_out_weight = lax.psum(partial_value, ('dp', 'seq')) * grad_scale  187 us
    dot_general x16, matrix products, table_apply(): return jnp.einsum(pattern, matrix, values, precision=lax.Precision.HIGHEST)  59.4 us
    ppermute x24, starting transfers between devices, swapped(): lax.ppermute(array, axis, [(i, i ^ 1 << apart) for i in range(lax.axis_si...  25.7 us
  transfers between devices with their start and end apart: 28, of which 20 were waited for; matrix products, arithmetic and copies ran while one was open for 6% of the time, Pallas kernels for 0%

profile of v1, /device:TPU:1, one launch (start us, length us, event | category | flops | bytes accessed | tf_op | source)
XLA Modules:
  0.0 1072.9 jit_solution(11540240948079647801)
XLA Ops:
  31.8 36.8 %collective-permute-done.2 = f32[4,256,512]{2,1,0:T(8,128)} collective-permute-done((f32[4,256,512]{2,1,0:T(8,128)}, f32[4,256,512]{2,1,0:T(8,128)}, u32[]{:S(2)}, u32[]{:S(2)}) %collective-permute-start.2) | collective-permute-done | bytes 2097184 | tf_op jit(solution)/shard_map/ppermute | solution.py:9
  68.6 44.9 %collective-permute-done.1 = f32[4,256,512]{2,1,0:T(8,128)} collective-permute-done((f32[4,256,512]{2,1,0:T(8,128)}, f32[4,256,512]{2,1,0:T(8,128)}, u32[]{:S(2)}, u32[]{:S(2)}) %collective-permute-start.1) | collective-permute-done | bytes 2097184 | tf_op jit(solution)/shard_map/ppermute | solution.py:9
  113.6 6.2 add_select_fusion.9
  121.2 14.8 %collective-permute-done.14 = f32[2,256,512]{2,1,0:T(8,128)} collective-permute-done((f32[2,256,512]{2,1,0:T(8,128)}, f32[2,256,512]{2,1,0:T(8,128)}, u32[]{:S(2)}, u32[]{:S(2)}) %collective-permute-start.14) | collective-permute-done | bytes 1048608 | tf_op jit(solution)/shard_map/ppermute | solution.py:9
  136.0 22.5 %collective-permute-done.13 = f32[2,256,512]{2,1,0:T(8,128)} collective-permute-done((f32[2,256,512]{2,1,0:T(8,128)}, f32[2,256,512]{2,1,0:T(8,128)}, u32[]{:S(2)}, u32[]{:S(2)}) %collective-permute-start.13) | collective-permute-done | bytes 1048608 | tf_op jit(solution)/shard_map/ppermute | solution.py:9
  163.4 107.4 %collective-permute-done.16 = f32[2,256,512]{2,1,0:T(8,128)} collective-permute-done((f32[2,256,512]{2,1,0:T(8,128)}, f32[2,256,512]{2,1,0:T(8,128)}, u32[]{:S(2)}, u32[]{:S(2)}) %collective-permute-start.16) | collective-permute-done | bytes 1048608 | tf_op jit(solution)/shard_map/ppermute | solution.py:9
  270.9 22.5 %collective-permute-done.15 = f32[2,256,512]{2,1,0:T(8,128)} collective-permute-done((f32[2,256,512]{2,1,0:T(8,128)}, f32[2,256,512]{2,1,0:T(8,128)}, u32[]{:S(2)}, u32[]{:S(2)}) %collective-permute-start.15) | collective-permute-done | bytes 1048608 | tf_op jit(solution)/shard_map/ppermute | solution.py:9
  298.9 6.7 add_select_fusion.7
  307.6 12.1 %collective-permute-done.18 = f32[2,256,512]{2,1,0:T(8,128)} collective-permute-done((f32[2,256,512]{2,1,0:T(8,128)}, f32[2,256,512]{2,1,0:T(8,128)}, u32[]{:S(2)}, u32[]{:S(2)}) %collective-permute-start.18) | collective-permute-done | bytes 1048608 | tf_op jit(solution)/shard_map/ppermute | solution.py:9
  319.7 22.5 %collective-permute-done.17 = f32[2,256,512]{2,1,0:T(8,128)} collective-permute-done((f32[2,256,512]{2,1,0:T(8,128)}, f32[2,256,512]{2,1,0:T(8,128)}, u32[]{:S(2)}, u32[]{:S(2)}) %collective-permute-start.17) | collective-permute-done | bytes 1048608 | tf_op jit(solution)/shard_map/ppermute | solution.py:9
  352.9 34.2 %collective-permute-done.5 = f32[4,256,512]{2,1,0:T(8,128)} collective-permute-done((f32[4,256,512]{2,1,0:T(8,128)}, f32[4,256,512]{2,1,0:T(8,128)}, u32[]{:S(2)}, u32[]{:S(2)}) %collective-permute-start.5) | collective-permute-done | bytes 2097184 | tf_op jit(solution)/shard_map/ppermute | solution.py:9
  387.1 44.9 %collective-permute-done.6 = f32[4,256,512]{2,1,0:T(8,128)} collective-permute-done((f32[4,256,512]{2,1,0:T(8,128)}, f32[4,256,512]{2,1,0:T(8,128)}, u32[]{:S(2)}, u32[]{:S(2)}) %collective-permute-start.6) | collective-permute-done | bytes 2097184 | tf_op jit(solution)/shard_map/ppermute | solution.py:9
  455.1 6.3 multiply_subtract_fusion.2
  496.7 35.5 %collective-permute-done.20 = f32[4,256,512]{2,1,0:T(8,128)S(1)} collective-permute-done((f32[4,256,512]{2,1,0:T(8,128)S(1)}, f32[4,256,512]{2,1,0:T(8,128)S(1)}, u32[]{:S(2)}, u32[]{:S(2)}) %collective-permute-start.20) | collective-permute-done | bytes 2097184 | tf_op jit(solution)/shard_map/ppermute | solution.py:9
  532.2 44.9 %collective-permute-done.19 = f32[4,256,512]{2,1,0:T(8,128)S(1)} collective-permute-done((f32[4,256,512]{2,1,0:T(8,128)S(1)}, f32[4,256,512]{2,1,0:T(8,128)S(1)}, u32[]{:S(2)}, u32[]{:S(2)}) %collective-permute-start.19) | collective-permute-done | bytes 2097184 | tf_op jit(solution)/shard_map/ppermute | solution.py:9
  584.2 18.0 %collective-permute-done.8 = f32[2,256,512]{2,1,0:T(8,128)S(1)} collective-permute-done((f32[2,256,512]{2,1,0:T(8,128)S(1)}, f32[2,256,512]{2,1,0:T(8,128)S(1)}, u32[]{:S(2)}, u32[]{:S(2)}) %collective-permute-start.8) | collective-permute-done | bytes 1048608 | tf_op jit(solution)/shard_map/ppermute | solution.py:9
  602.2 22.5 %collective-permute-done.7 = f32[2,256,512]{2,1,0:T(8,128)S(1)} collective-permute-done((f32[2,256,512]{2,1,0:T(8,128)S(1)}, f32[2,256,512]{2,1,0:T(8,128)S(1)}, u32[]{:S(2)}, u32[]{:S(2)}) %collective-permute-start.7) | collective-permute-done | bytes 1048608 | tf_op jit(solution)/shard_map/ppermute | solution.py:9
  627.1 39.0 %collective-permute-done.21 = f32[4,256,512]{2,1,0:T(8,128)S(1)} collective-permute-done((f32[4,256,512]{2,1,0:T(8,128)S(1)}, f32[4,256,512]{2,1,0:T(8,128)S(1)}, u32[]{:S(2)}, u32[]{:S(2)}) %collective-permute-start.21) | collective-permute-done | bytes 2097184 | tf_op jit(solution)/shard_map/ppermute | solution.py:9
  670.7 17.9 %collective-permute-done.10 = f32[2,256,512]{2,1,0:T(8,128)S(1)} collective-permute-done((f32[2,256,512]{2,1,0:T(8,128)S(1)}, f32[2,256,512]{2,1,0:T(8,128)S(1)}, u32[]{:S(2)}, u32[]{:S(2)}) %collective-permute-start.10) | collective-permute-done | bytes 1048608 | tf_op jit(solution)/shard_map/ppermute | solution.py:9
  688.6 22.5 %collective-permute-done.9 = f32[2,256,512]{2,1,0:T(8,128)S(1)} collective-permute-done((f32[2,256,512]{2,1,0:T(8,128)S(1)}, f32[2,256,512]{2,1,0:T(8,128)S(1)}, u32[]{:S(2)}, u32[]{:S(2)}) %collective-permute-start.9) | collective-permute-done | bytes 1048608 | tf_op jit(solution)/shard_map/ppermute | solution.py:9
  714.9 109.4 %collective-permute-done.11 = f32[2,256,512]{2,1,0:T(8,128)S(1)} collective-permute-done((f32[2,256,512]{2,1,0:T(8,128)S(1)}, f32[2,256,512]{2,1,0:T(8,128)S(1)}, u32[]{:S(2)}, u32[]{:S(2)}) %collective-permute-start.11) | collective-permute-done | bytes 1048608 | tf_op jit(solution)/shard_map/ppermute | solution.py:9
  824.5 22.2 %collective-permute-done.12 = f32[2,256,512]{2,1,0:T(8,128)S(1)} collective-permute-done((f32[2,256,512]{2,1,0:T(8,128)S(1)}, f32[2,256,512]{2,1,0:T(8,128)S(1)}, u32[]{:S(2)}, u32[]{:S(2)}) %collective-permute-start.12) | collective-permute-done | bytes 1048608 | tf_op jit(solution)/shard_map/ppermute | solution.py:9
  864.8 186.9 %all-reduce.4.cloned.1.call-done = f32[512,4096]{1,0:T(8,128)} async-done(((f32[512,4096]{1,0:T(8,128)}), f32[512,4096]{1,0:T(8,128)}) %all-reduce.4.cloned.1.call-update) | async-done | bytes 8388624 | tf_op jit(solution)/shard_map/psum | solution.py:215
  1051.7 8.3 broadcast_multiply_fusion
  (147 shorter events, 147.7 us)
Async XLA Ops:
  8.0 1043.7 %all-reduce.4.cloned.1.call-start = ((), (), s32[]{:S(2)}) async-start(), calls=%async_computation.1 | async-start | bytes 16777216 | tf_op jit(solution)/shard_map/psum | solution.py:215
  20.4 48.2 %collective-permute-start.2 = (f32[4,256,512]{2,1,0:T(8,128)}, f32[4,256,512]{2,1,0:T(8,128)}, u32[]{:S(2)}, u32[]{:S(2)}) collective-permute-start(f32[4,256,512]{2,1,0:T(8,128)} %concatenate.47), channel_id=1, source_target_pairs={{0,4},{1,5},{2,6},{3,7},{4,0},{5,1},{6,2},{7,3},{8,12},{9,13},{10,... | collective-permute-start | bytes 6291464 | tf_op jit(solution)/shard_map/ppermute | solution.py:9
  24.2 89.4 %collective-permute-start.1 = (f32[4,256,512]{2,1,0:T(8,128)}, f32[4,256,512]{2,1,0:T(8,128)}, u32[]{:S(2)}, u32[]{:S(2)}) collective-permute-start(f32[4,256,512]{2,1,0:T(8,128)} %pad_maximum_fusion), channel_id=1, source_target_pairs={{0,4},{1,5},{2,6},{3,7},{4,0},{5,1},{6,2},{7,3},{8,12},{9,13},{10,... | collective-permute-start | bytes 6291464 | tf_op jit(solution)/shard_map/ppermute | solution.py:9
  26.8 109.2 %collective-permute-start.14 = (f32[2,256,512]{2,1,0:T(8,128)}, f32[2,256,512]{2,1,0:T(8,128)}, u32[]{:S(2)}, u32[]{:S(2)}) collective-permute-start(f32[2,256,512]{2,1,0:T(8,128)} %concatenate.49), channel_id=1, source_target_pairs={{0,4},{1,5},{2,6},{3,7},{4,0},{5,1},{6,2},{7,3},{8,12},{9,13},{10,... | collective-permute-start | bytes 3145736 | tf_op jit(solution)/shard_map/ppermute | solution.py:9
  31.7 126.7 %collective-permute-start.13 = (f32[2,256,512]{2,1,0:T(8,128)}, f32[2,256,512]{2,1,0:T(8,128)}, u32[]{:S(2)}, u32[]{:S(2)}) collective-permute-start(f32[2,256,512]{2,1,0:T(8,128)} %pad_maximum_fusion.6), channel_id=1, source_target_pairs={{0,4},{1,5},{2,6},{3,7},{4,0},{5,1},{6,2},{7,3},{8,12},{9,13},{10,... | collective-permute-start | bytes 3145736 | tf_op jit(solution)/shard_map/ppermute | solution.py:9
  119.8 179.2 %collective-permute-start.3 = (f32[4,256,512]{2,1,0:T(8,128)}, f32[4,256,512]{2,1,0:T(8,128)}, u32[]{:S(2)}, u32[]{:S(2)}) collective-permute-start(f32[4,256,512]{2,1,0:T(8,128)} %get-tuple-element.16), channel_id=1, source_target_pairs={{0,2},{1,3},{2,0},{3,1},{4,6},{5,7},{6,4},{7,5},{8,10},{9,11},{10,... | collective-permute-start | bytes 6291464 | tf_op jit(solution)/shard_map/ppermute | solution.py:9
  120.9 178.0 %collective-permute-start.4 = (f32[4,256,512]{2,1,0:T(8,128)}, f32[4,256,512]{2,1,0:T(8,128)}, u32[]{:S(2)}, u32[]{:S(2)}) collective-permute-start(f32[4,256,512]{2,1,0:T(8,128)} %get-tuple-element.17), channel_id=1, source_target_pairs={{0,2},{1,3},{2,0},{3,1},{4,6},{5,7},{6,4},{7,5},{8,10},{9,11},{10,... | collective-permute-start | bytes 6291464 | tf_op jit(solution)/shard_map/ppermute | solution.py:9
  161.9 109.0 %collective-permute-start.16 = (f32[2,256,512]{2,1,0:T(8,128)}, f32[2,256,512]{2,1,0:T(8,128)}, u32[]{:S(2)}, u32[]{:S(2)}) collective-permute-start(f32[2,256,512]{2,1,0:T(8,128)} %get-tuple-element.34), channel_id=1, source_target_pairs={{0,2},{1,3},{2,0},{3,1},{4,6},{5,7},{6,4},{7,5},{8,10},{9,11},{10,... | collective-permute-start | bytes 3145736 | tf_op jit(solution)/shard_map/ppermute | solution.py:9
  163.1 130.3 %collective-permute-start.15 = (f32[2,256,512]{2,1,0:T(8,128)}, f32[2,256,512]{2,1,0:T(8,128)}, u32[]{:S(2)}, u32[]{:S(2)}) collective-permute-start(f32[2,256,512]{2,1,0:T(8,128)} %get-tuple-element.35), channel_id=1, source_target_pairs={{0,2},{1,3},{2,0},{3,1},{4,6},{5,7},{6,4},{7,5},{8,10},{9,11},{10,... | collective-permute-start | bytes 3145736 | tf_op jit(solution)/shard_map/ppermute | solution.py:9
  297.9 44.3 %collective-permute-start.17 = (f32[2,256,512]{2,1,0:T(8,128)}, f32[2,256,512]{2,1,0:T(8,128)}, u32[]{:S(2)}, u32[]{:S(2)}) collective-permute-start(f32[2,256,512]{2,1,0:T(8,128)} %get-tuple-element.27), channel_id=1, source_target_pairs={{0,1},{1,0},{2,3},{3,2},{4,5},{5,4},{6,7},{7,6},{8,9},{9,8},{10,11... | collective-permute-start | bytes 3145736 | tf_op jit(solution)/shard_map/ppermute | solution.py:9
  305.6 81.5 %collective-permute-start.5 = (f32[4,256,512]{2,1,0:T(8,128)}, f32[4,256,512]{2,1,0:T(8,128)}, u32[]{:S(2)}, u32[]{:S(2)}) collective-permute-start(f32[4,256,512]{2,1,0:T(8,128)} %get-tuple-element.14), channel_id=1, source_target_pairs={{0,1},{1,0},{2,3},{3,2},{4,5},{5,4},{6,7},{7,6},{8,9},{9,8},{10,11... | collective-permute-start | bytes 6291464 | tf_op jit(solution)/shard_map/ppermute | solution.py:9
  306.0 126.0 %collective-permute-start.6 = (f32[4,256,512]{2,1,0:T(8,128)}, f32[4,256,512]{2,1,0:T(8,128)}, u32[]{:S(2)}, u32[]{:S(2)}) collective-permute-start(f32[4,256,512]{2,1,0:T(8,128)} %get-tuple-element.15), channel_id=1, source_target_pairs={{0,1},{1,0},{2,3},{3,2},{4,5},{5,4},{6,7},{7,6},{8,9},{9,8},{10,11... | collective-permute-start | bytes 6291464 | tf_op jit(solution)/shard_map/ppermute | solution.py:9
  488.6 43.5 %collective-permute-start.20 = (f32[4,256,512]{2,1,0:T(8,128)S(1)}, f32[4,256,512]{2,1,0:T(8,128)S(1)}, u32[]{:S(2)}, u32[]{:S(2)}) collective-permute-start(f32[4,256,512]{2,1,0:T(8,128)S(1)} %get-tuple-element.22), channel_id=1, source_target_pairs={{0,1},{1,0},{2,3},{3,2},{4,5},{5,4},{6,7},{7,6},{8,9},{9,8},{10,11... | collective-permute-start | bytes 6291464 | tf_op jit(solution)/shard_map/ppermute | solution.py:9
  489.1 88.0 %collective-permute-start.19 = (f32[4,256,512]{2,1,0:T(8,128)S(1)}, f32[4,256,512]{2,1,0:T(8,128)S(1)}, u32[]{:S(2)}, u32[]{:S(2)}) collective-permute-start(f32[4,256,512]{2,1,0:T(8,128)S(1)} %get-tuple-element.23), channel_id=1, source_target_pairs={{0,1},{1,0},{2,3},{3,2},{4,5},{5,4},{6,7},{7,6},{8,9},{9,8},{10,11... | collective-permute-start | bytes 6291464 | tf_op jit(solution)/shard_map/ppermute | solution.py:9
  578.6 48.5 %collective-permute-start.22 = (f32[4,256,512]{2,1,0:T(8,128)S(1)}, f32[4,256,512]{2,1,0:T(8,128)S(1)}, u32[]{:S(2)}, u32[]{:S(2)}) collective-permute-start(f32[4,256,512]{2,1,0:T(8,128)S(1)} %get-tuple-element.10), channel_id=1, source_target_pairs={{0,2},{1,3},{2,0},{3,1},{4,6},{5,7},{6,4},{7,5},{8,10},{9,11},{10,... | collective-permute-start | bytes 6291464 | tf_op jit(solution)/shard_map/ppermute | solution.py:9
  579.9 86.3 %collective-permute-start.21 = (f32[4,256,512]{2,1,0:T(8,128)S(1)}, f32[4,256,512]{2,1,0:T(8,128)S(1)}, u32[]{:S(2)}, u32[]{:S(2)}) collective-permute-start(f32[4,256,512]{2,1,0:T(8,128)S(1)} %get-tuple-element.11), channel_id=1, source_target_pairs={{0,2},{1,3},{2,0},{3,1},{4,6},{5,7},{6,4},{7,5},{8,10},{9,11},{10,... | collective-permute-start | bytes 6291464 | tf_op jit(solution)/shard_map/ppermute | solution.py:9
  583.1 41.6 %collective-permute-start.7 = (f32[2,256,512]{2,1,0:T(8,128)S(1)}, f32[2,256,512]{2,1,0:T(8,128)S(1)}, u32[]{:S(2)}, u32[]{:S(2)}) collective-permute-start(f32[2,256,512]{2,1,0:T(8,128)S(1)} %get-tuple-element.39), channel_id=1, source_target_pairs={{0,1},{1,0},{2,3},{3,2},{4,5},{5,4},{6,7},{7,6},{8,9},{9,8},{10,11... | collective-permute-start | bytes 3145736 | tf_op jit(solution)/shard_map/ppermute | solution.py:9
  625.3 63.3 %collective-permute-start.10 = (f32[2,256,512]{2,1,0:T(8,128)S(1)}, f32[2,256,512]{2,1,0:T(8,128)S(1)}, u32[]{:S(2)}, u32[]{:S(2)}) collective-permute-start(f32[2,256,512]{2,1,0:T(8,128)S(1)} %get-tuple-element.30), channel_id=1, source_target_pairs={{0,2},{1,3},{2,0},{3,1},{4,6},{5,7},{6,4},{7,5},{8,10},{9,11},{10,... | collective-permute-start | bytes 3145736 | tf_op jit(solution)/shard_map/ppermute | solution.py:9
  626.8 84.3 %collective-permute-start.9 = (f32[2,256,512]{2,1,0:T(8,128)S(1)}, f32[2,256,512]{2,1,0:T(8,128)S(1)}, u32[]{:S(2)}, u32[]{:S(2)}) collective-permute-start(f32[2,256,512]{2,1,0:T(8,128)S(1)} %get-tuple-element.31), channel_id=1, source_target_pairs={{0,2},{1,3},{2,0},{3,1},{4,6},{5,7},{6,4},{7,5},{8,10},{9,11},{10,... | collective-permute-start | bytes 3145736 | tf_op jit(solution)/shard_map/ppermute | solution.py:9
  667.6 180.2 %collective-permute-start.23 = (f32[4,256,512]{2,1,0:T(8,128)S(1)}, f32[4,256,512]{2,1,0:T(8,128)S(1)}, u32[]{:S(2)}, u32[]{:S(2)}) collective-permute-start(f32[4,256,512]{2,1,0:T(8,128)S(1)} %get-tuple-element.9), channel_id=1, source_target_pairs={{0,4},{1,5},{2,6},{3,7},{4,0},{5,1},{6,2},{7,3},{8,12},{9,13},{10,... | collective-permute-start | bytes 6291464 | tf_op jit(solution)/shard_map/ppermute | solution.py:9
  669.5 178.9 %collective-permute-start.24 = (f32[4,256,512]{2,1,0:T(8,128)S(1)}, f32[4,256,512]{2,1,0:T(8,128)S(1)}, u32[]{:S(2)}, u32[]{:S(2)}) collective-permute-start(f32[4,256,512]{2,1,0:T(8,128)S(1)} %get-tuple-element.8), channel_id=1, source_target_pairs={{0,4},{1,5},{2,6},{3,7},{4,0},{5,1},{6,2},{7,3},{8,12},{9,13},{10,... | collective-permute-start | bytes 6291464 | tf_op jit(solution)/shard_map/ppermute | solution.py:9
  711.8 112.5 %collective-permute-start.11 = (f32[2,256,512]{2,1,0:T(8,128)S(1)}, f32[2,256,512]{2,1,0:T(8,128)S(1)}, u32[]{:S(2)}, u32[]{:S(2)}) collective-permute-start(f32[2,256,512]{2,1,0:T(8,128)S(1)} %get-tuple-element.28), channel_id=1, source_target_pairs={{0,4},{1,5},{2,6},{3,7},{4,0},{5,1},{6,2},{7,3},{8,12},{9,13},{10,... | collective-permute-start | bytes 3145736 | tf_op jit(solution)/shard_map/ppermute | solution.py:9
  713.6 133.1 %collective-permute-start.12 = (f32[2,256,512]{2,1,0:T(8,128)S(1)}, f32[2,256,512]{2,1,0:T(8,128)S(1)}, u32[]{:S(2)}, u32[]{:S(2)}) collective-permute-start(f32[2,256,512]{2,1,0:T(8,128)S(1)} %get-tuple-element.29), channel_id=1, source_target_pairs={{0,4},{1,5},{2,6},{3,7},{4,0},{5,1},{6,2},{7,3},{8,12},{9,13},{10,... | collective-permute-start | bytes 3145736 | tf_op jit(solution)/shard_map/ppermute | solution.py:9
  854.8 205.1 %all-gather.2.cloned.1.call-start = ((), (), s32[]{:S(2)}) async-start(), calls=%async_computation | async-start | bytes 8912896 | tf_op jit(solution)/shard_map/all_gather | solution.py:216
  (27 other events, 637.2 us)
Sparse Core Ops, SparseCore 0:
  854.9 196.7 all-reduce.3
Sparse Core Ops, SparseCore 1:
  857.8 80.6 all-gather.1
